TPU v7x, 32 devices: a whole 2x2x4 slice. The times are simulated.
32 devices in a mesh: ep: 16 (over z, y, x), dp: 2 (over core).
Axes of the slice: x: 2, y: 2, z: 4, core: 2. Of those that a mesh axis runs over, the one named last changes fastest.
Arguments:
- tokens: bfloat16 [4096, 1024], P(('ep', 'dp')), may hold values from -6 to 6
- grad_out: bfloat16 [4096, 1024], P(('ep', 'dp')), may hold values from -3 to 3
- assign: int32 [4096, 2], P(('ep', 'dp')), may hold values from 0 to 15, as said below
- router_weight: bfloat16 [16, 1024], P('ep'), may hold values from -0.1875 to 0.1875
- w_gate: bfloat16 [16, 1024, 2048], P('ep', None, 'dp'), may hold values from -0.1875 to 0.1875
- w_up: bfloat16 [16, 1024, 2048], P('ep', None, 'dp'), may hold values from -0.1875 to 0.1875
- w_down: bfloat16 [16, 2048, 1024], P('ep', 'dp'), may hold values from -0.125 to 0.125
Outputs:
- grad_tokens: bfloat16 [4096, 1024], P(('ep', 'dp'))
- grad_router: float32 [16, 1024], P('ep')
- grad_gate: bfloat16 [16, 1024, 2048], P('ep', None, 'dp')
- grad_up: bfloat16 [16, 1024, 2048], P('ep', None, 'dp')
- grad_down: bfloat16 [16, 2048, 1024], P('ep', 'dp')
Inputs may be any that keep to these rules, and one draw needn't show every extreme that they name: `assign`: in each aligned block of 128 rows (the rows of one device) the two experts of a row differ and no expert is named by more than 24 entries; in every block one expert, the same for all blocks, is named by exactly 24 entries.
All inputs are finite; a program needn't handle non-finite values.
Results may differ from a plain program's by a relative error of at most 0.007.
Values may be sent and summed in bfloat16 or wider, within the bound.
A program may use at most 192 MiB of HBM per device.

v0:
```python
import jax
import jax.numpy as jnp
from jax import lax
from jax.sharding import PartitionSpec as P


def entry_slots(assign, experts, cap):
    flat = assign.reshape(-1)
    marks = (flat[:, None] == jnp.arange(experts, dtype=jnp.int32)[None, :]).astype(jnp.int32)
    before = jnp.cumsum(marks, axis=0) - marks
    ranks = jnp.sum(before * marks, axis=1)
    return flat * cap + ranks


def expert_grads(rows, upstream, gate_vals, wg, wu, wd):
    pre_a = jnp.dot(rows, wg, preferred_element_type=jnp.float32)
    pre_b = jnp.dot(rows, wu, preferred_element_type=jnp.float32)
    sigma = jax.nn.sigmoid(pre_a)
    active = pre_a * sigma
    hidden = (active * pre_b).astype(jnp.bfloat16)
    outer = jnp.dot(hidden, wd, preferred_element_type=jnp.float32)
    up_f = upstream.astype(jnp.float32)
    grad_gates = jnp.sum(up_f * outer, axis=1)
    scaled = (gate_vals.astype(jnp.float32)[:, None] * up_f).astype(jnp.bfloat16)
    grad_hidden = jnp.dot(scaled, wd.T, preferred_element_type=jnp.float32)
    grad_a = (grad_hidden * pre_b * sigma * (1.0 + pre_a * (1.0 - sigma))).astype(jnp.bfloat16)
    grad_b = (grad_hidden * active).astype(jnp.bfloat16)
    grad_rows = jnp.dot(grad_a, wg.T, preferred_element_type=jnp.float32) + jnp.dot(
        grad_b, wu.T, preferred_element_type=jnp.float32
    )
    g_gate = jnp.dot(rows.T, grad_a, preferred_element_type=jnp.float32)
    g_up = jnp.dot(rows.T, grad_b, preferred_element_type=jnp.float32)
    g_down = jnp.dot(hidden.T, scaled, preferred_element_type=jnp.float32)
    return (grad_rows, grad_gates, g_gate, g_up, g_down)


def local(tokens, grad_out, assign, router_weight, w_gate, w_up, w_down):
    tok_rows = tokens.shape[0]
    width = tokens.shape[1]
    router_full = lax.all_gather(router_weight, "ep", axis=0, tiled=True)
    experts = router_full.shape[0]
    cap = max(2, (3 * tok_rows + experts - 1) // experts)
    choose = (assign[:, :, None] == jnp.arange(experts, dtype=jnp.int32)[None, None, :]).astype(
        jnp.float32
    )
    scores = jnp.dot(tokens, router_full.T, preferred_element_type=jnp.float32)
    picked = jnp.sum(scores[:, None, :] * choose, axis=2)
    sig = jax.nn.sigmoid(picked)
    total = jnp.sum(sig, axis=1, keepdims=True)
    gates = sig / total
    slots = entry_slots(assign, experts, cap)
    entries = 2 * tok_rows
    table = (
        jnp.full((experts * cap,), -1, dtype=jnp.int32)
        .at[slots]
        .set(jnp.arange(entries, dtype=jnp.int32))
    )
    valid = table >= 0
    safe = jnp.maximum(table, 0)
    zero_low = jnp.zeros((), jnp.bfloat16)
    send_rows = jnp.where(valid[:, None], tokens[safe // 2], zero_low).reshape(experts, cap, width)
    send_ups = jnp.where(valid[:, None], grad_out[safe // 2], zero_low).reshape(experts, cap, width)
    send_gates = (
        jnp.where(valid, gates.reshape(-1)[safe], 0.0).astype(jnp.bfloat16).reshape(experts, cap)
    )
    got_rows, got_ups, got_gates = (
        lax.all_to_all(send_rows, "ep", split_axis=0, concat_axis=0, tiled=True),
        lax.all_to_all(send_ups, "ep", split_axis=0, concat_axis=0, tiled=True),
        lax.all_to_all(send_gates, "ep", split_axis=0, concat_axis=0, tiled=True),
    )
    rows = got_rows.reshape(experts * cap, width)
    ups = got_ups.reshape(experts * cap, width)
    gts = got_gates.reshape(experts * cap)
    both_rows, both_ups, both_gates = (
        lax.all_gather(rows, "dp", axis=0, tiled=True),
        lax.all_gather(ups, "dp", axis=0, tiled=True),
        lax.all_gather(gts, "dp", axis=0, tiled=True),
    )
    part_rows, part_gates, g_gate, g_up, g_down = expert_grads(
        both_rows, both_ups, both_gates, w_gate[0], w_up[0], w_down[0]
    )
    grad_rows, grad_gates = (
        lax.psum_scatter(part_rows, "dp", scatter_dimension=0, tiled=True),
        lax.psum_scatter(part_gates, "dp", scatter_dimension=0, tiled=True),
    )
    grad_gate = g_gate.astype(jnp.bfloat16)[None]
    grad_up = g_up.astype(jnp.bfloat16)[None]
    grad_down = g_down.astype(jnp.bfloat16)[None]
    back_rows, back_gates = (
        lax.all_to_all(
            grad_rows.astype(jnp.bfloat16).reshape(experts, cap, width),
            "ep",
            split_axis=0,
            concat_axis=0,
            tiled=True,
        ),
        lax.all_to_all(
            grad_gates.astype(jnp.bfloat16).reshape(experts, cap),
            "ep",
            split_axis=0,
            concat_axis=0,
            tiled=True,
        ),
    )
    entry_rows = (
        back_rows.reshape(experts * cap, width)[slots]
        .astype(jnp.float32)
        .reshape(tok_rows, 2, width)
    )
    entry_gates = back_gates.reshape(experts * cap)[slots].astype(jnp.float32).reshape(tok_rows, 2)
    mixed = jnp.sum(gates * entry_gates, axis=1, keepdims=True)
    grad_logit = (entry_gates - mixed) / total * sig * (1.0 - sig)
    dense = jnp.sum(grad_logit[:, :, None] * choose, axis=1)
    router_term = jnp.dot(dense, router_full.astype(jnp.float32), precision=lax.Precision.HIGHEST)
    grad_tokens = (jnp.sum(entry_rows, axis=1) + router_term).astype(jnp.bfloat16)
    partial_router = jnp.dot(dense.T, tokens.astype(jnp.float32), precision=lax.Precision.HIGHEST)
    summed = lax.psum(partial_router, ("ep", "dp"))
    grad_router = lax.dynamic_slice_in_dim(summed, lax.axis_index("ep"), 1, 0)
    return (grad_tokens, grad_router, grad_gate, grad_up, grad_down)


def solution(mesh):
    return jax.shard_map(
        local,
        mesh=mesh,
        in_specs=(
            P(("ep", "dp"), None),
            P(("ep", "dp"), None),
            P(("ep", "dp"), None),
            P("ep", None),
            P("ep", None, "dp"),
            P("ep", None, "dp"),
            P("ep", "dp", None),
        ),
        out_specs=(
            P(("ep", "dp"), None),
            P("ep", None),
            P("ep", None, "dp"),
            P("ep", None, "dp"),
            P("ep", "dp", None),
        ),
        check_vma=False,
    )
```

profile of v0, /device:TPU:1, one launch (start us, length us, event | category | flops | bytes accessed | tf_op | source)
XLA Modules:
  0.0 320.5 jit_solution(11369833928976403874)
XLA Ops:
  14.0 2.7 gather_fusion.2
  16.7 2.2 broadcast_select_fusion.1
  18.9 27.4 %all_to_all.35 = bf16[16,24,1024]{2,1,0:T(8,128)(2,1)} all-to-all(bf16[16,24,1024]{2,1,0:T(8,128)(2,1)S(1)} %get-tuple-element.14), channel_id=1, replica_groups=mesh['ep'=16,'dp'=2] {'ep'}, dimensions={0} | all-to-all | bytes 1572864 | tf_op jit(solution)/shard_map/all_to_all | solution.py:67
  46.4 4.1 %all-to-all-start.1 = ((bf16[16,24,1024]{2,1,0:T(8,128)(2,1)}), bf16[16,24,1024]{2,1,0:T(8,128)(2,1)S(1)}, u32[]{:S(2)}, u32[]{:S(2)}) async-start(bf16[16,24,1024]{2,1,0:T(8,128)(2,1)} %get-tuple-element.13), calls=%async_computation.1 | async-start | bytes 1572864 | tf_op jit(solution)/shard_map/all_to_all | solution.py:68
  50.5 39.2 %all-gather = bf16[16,1,1024]{2,1,0:T(2,128)(2,1)S(1)} all-gather(bf16[1,1,1024]{2,1,0:T(2,128)(2,1)S(1)} %bitcast.83), channel_id=1, replica_groups=mesh['ep'=16,'dp'=2] {'ep'}, dimensions={0}, use_global_device_ids=true | all-gather | bytes 34816 | tf_op jit(solution)/shard_map/all_gather | solution.py:40
  92.1 4.0 %fusion.5 = f32[768,1024]{1,0:T(8,128)S(1)} fusion(bf16[768,1024]{1,0:T(8,128)(2,1)} %all-gather.7.cloned.1.call-done, bf16[1,1024,1024]{2,1,0:T(8,128)(2,1)} %param.11), kind=kOutput, calls=%fused_computation.17 | convolution fusion | flops 1610612736 | bytes 6815744 | tf_op jit(solution)/shard_map/dot_general | solution.py:16
  97.8 4.2 %multiply_convert_fusion = (bf16[768,1024]{1,0:T(8,128)(2,1)}, f32[768,1024]{1,0:T(8,128)}) fusion(f32[768,1024]{1,0:T(8,128)S(1)} %fusion.5, bf16[768,1024]{1,0:T(8,128)(2,1)S(1)} %copy-done.7, bf16[1,1024,1024]{2,1,0:T(8,128)(2,1)S(1)} %copy-done), kind=kOutput, calls=%fused_computation.10 | convolution fusion | flops 1615331328 | bytes 11534336 | tf_op jit(solution)/shard_map/dot_general | solution.py:17
  102.0 4.8 %all-gather.5.cloned.1.call-done = bf16[768,1024]{1,0:T(8,128)(2,1)} async-done(((bf16[384,1024]{1,0:T(8,128)(2,1)}), bf16[768,1024]{1,0:T(8,128)(2,1)}) %all-gather.5.cloned.1.call-update) | async-done | bytes 1572880 | tf_op jit(solution)/shard_map/all_gather | solution.py:76
  106.8 4.4 %fusion.1 = f32[768]{0:T(1024)S(1)} fusion(bf16[768,1024]{1,0:T(8,128)(2,1)} %all-gather.5.cloned.1.call-done, bf16[768,1024]{1,0:T(8,128)(2,1)} %get-tuple-element.15, bf16[1,1024,1024]{2,1,0:T(8,128)(2,1)} %param.13), kind=kOutput, calls=%fused_computation.9 | convolution fusion | flops 1612971264 | bytes 5245952 | tf_op jit(solution)/shard_map/dot_general | solution.py:21
  111.1 6.0 %all-reduce = bf16[768]{0:T(1024)(128)(2,1)S(1)} all-reduce(f32[768]{0:T(1024)S(1)} %fusion.1), channel_id=3, replica_groups=mesh['ep'=16,'dp'=2] {'dp'}, use_global_device_ids=true, to_apply=%region_9.10.clone | all-reduce | flops 768 | bytes 4608
  117.9 3.5 %all-to-all-start.4 = ((bf16[16,1,24]{2,1,0:T(2,128)(2,1)}), bf16[16,1,24]{2,1,0:T(2,128)(2,1)S(1)}, u32[]{:S(2)}, u32[]{:S(2)}) async-start(bf16[16,1,24]{2,1,0:T(2,128)(2,1)} %all_to_all.29), calls=%async_computation.5 | async-start | bytes 16384 | tf_op jit(solution)/shard_map/all_to_all | solution.py:97
  121.5 6.0 %all-to-all-done.4 = bf16[16,1,24]{2,1,0:T(2,128)(2,1)S(1)} async-done(((bf16[16,1,24]{2,1,0:T(2,128)(2,1)}), bf16[16,1,24]{2,1,0:T(2,128)(2,1)S(1)}, u32[]{:S(2)}, u32[]{:S(2)}) %all-to-all-start.4) | async-done | bytes 800 | tf_op jit(solution)/shard_map/all_to_all | solution.py:97
  130.1 2.7 gather_fusion
  132.9 8.7 %all_to_all.36 = bf16[16,1,24]{2,1,0:T(2,128)(2,1)S(1)} all-to-all(bf16[16,1,24]{2,1,0:T(2,128)(2,1)S(1)} %all_to_all.28), channel_id=1, replica_groups=mesh['ep'=16,'dp'=2] {'ep'}, dimensions={0} | all-to-all | bytes 1536 | tf_op jit(solution)/shard_map/all_to_all | solution.py:69
  141.8 4.3 %all-gather.1 = bf16[2,1,384]{2,1,0:T(2,128)(2,1)S(1)} all-gather(bf16[1,1,384]{2,1,0:T(2,128)(2,1)S(1)} %reshape.229), channel_id=1, replica_groups=mesh['ep'=16,'dp'=2] {'dp'}, dimensions={0}, use_global_device_ids=true | all-gather | bytes 2304 | tf_op jit(solution)/shard_map/all_gather | solution.py:77
  146.1 6.8 %multiply_convert_fusion.1 = (bf16[768,1024]{1,0:T(8,128)(2,1)S(1)}, bf16[768,1024]{1,0:T(8,128)(2,1)S(1)}) fusion(f32[768,1024]{1,0:T(8,128)} %copy-done.11, f32[768,1024]{1,0:T(8,128)} %get-tuple-element.16, bf16[1,1024,1024]{2,1,0:T(8,128)(2,1)} %param.13, bf16[768,1024]{1,0:T(8,128)(2,1)} %all-gather.5.cloned.1.call-done, f32[768]{0:T(1024)S(1)} %reshape.231), kind=kOutput, calls=%fused_computation.11 | convolution fusion | flops 1623195648 | bytes 13110272 | tf_op jit(solution)/shard_map/dot_general | solution.py:25
  154.8 3.5 %fusion.15 = f32[768,1024]{1,0:T(8,128)} fusion(f32[768,1024]{1,0:T(8,128)S(1)} %fusion.3, bf16[768,1024]{1,0:T(8,128)(2,1)S(1)} %get-tuple-element.9, bf16[1,1024,1024]{2,1,0:T(8,128)(2,1)S(1)} %copy-done), kind=kOutput, calls=%fused_computation.30 | convolution fusion | flops 1611399168 | bytes 9961472 | tf_op jit(solution)/shard_map/dot_general | solution.py:28
  158.4 7.8 %reduce-scatter.2.cloned.1.call-done = f32[384,1024]{1,0:T(8,128)} async-done(((f32[768,1024]{1,0:T(8,128)}), f32[384,1024]{1,0:T(8,128)}) %reduce-scatter.2.cloned.1.call-update) | async-done | bytes 1572880 | tf_op jit(solution)/shard_map/reduce_scatter | solution.py:83
  166.2 2.4 convert_element_type.75
  168.6 6.4 %all-to-all-start.3 = ((bf16[16,24,1024]{2,1,0:T(8,128)(2,1)}), bf16[16,24,1024]{2,1,0:T(8,128)(2,1)S(1)}, u32[]{:S(2)}, u32[]{:S(2)}) async-start(bf16[16,24,1024]{2,1,0:T(8,128)(2,1)} %bitcast.80), calls=%async_computation.4 | async-start | bytes 1572864 | tf_op jit(solution)/shard_map/all_to_all | solution.py:90
  176.2 5.2 %convert_bitcast_fusion.2 = bf16[1,1024,1024]{2,1,0:T(8,128)(2,1)} fusion(bf16[768,1024]{1,0:T(8,128)(2,1)} %all-gather.7.cloned.1.call-done, bf16[768,1024]{1,0:T(8,128)(2,1)} %copy-done.14), kind=kOutput, calls=%fused_computation.29 | convolution fusion | flops 1611661312 | bytes 5242880 | tf_op jit(solution)/shard_map/dot_general | solution.py:31
  181.4 3.3 %convert_bitcast_fusion = bf16[1,1024,1024]{2,1,0:T(8,128)(2,1)} fusion(bf16[768,1024]{1,0:T(8,128)(2,1)S(1)} %copy-done.15, bf16[768,1024]{1,0:T(8,128)(2,1)S(1)} %copy-done.9, f32[768]{0:T(1024)S(1)} %reshape.231), kind=kOutput, calls=%fused_computation.27 | convolution fusion | flops 1614020608 | bytes 5245952 | tf_op jit(solution)/shard_map/dot_general | solution.py:33
  184.7 3.2 convert_bitcast_fusion.1
  187.8 116.8 %all-reduce.3.cloned.1.call-done = f32[16,1024]{1,0:T(8,128)} async-done(((f32[16,1024]{1,0:T(8,128)}), f32[16,1024]{1,0:T(8,128)}) %all-reduce.3.cloned.1.call-update) | async-done | bytes 65552 | tf_op jit(solution)/shard_map/psum | solution.py:117
  (93 shorter events, 26.2 us)
Async XLA Ops:
  7.2 90.6 %copy-start = (bf16[1,1024,1024]{2,1,0:T(8,128)(2,1)S(1)}, bf16[1,1024,1024]{2,1,0:T(8,128)(2,1)}, u32[]{:S(2)}) copy-start(bf16[1,1024,1024]{2,1,0:T(8,128)(2,1)} %param.12) | copy-start | bytes 6291460
  7.2 4.7 %copy-start.2 = (bf16[128,1024]{1,0:T(8,128)(2,1)S(1)}, bf16[128,1024]{1,0:T(8,128)(2,1)}, u32[]{:S(2)}) copy-start(bf16[128,1024]{1,0:T(8,128)(2,1)} %param.8) | copy-start | bytes 786436
  7.2 84.9 %all-gather.7.cloned.1.call-start = ((), (), s32[]{:S(2)}) async-start(), calls=%async_computation.7 | async-start | bytes 2359296 | tf_op jit(solution)/shard_map/all_gather | solution.py:75
  11.9 2.1 copy-start.1
  18.9 31.7 %copy-start.5 = (bf16[1,1024]{1,0:T(2,128)(2,1)S(1)}, bf16[1,1024]{1,0:T(2,128)(2,1)}, u32[]{:S(2)}) copy-start(bf16[1,1024]{1,0:T(2,128)(2,1)} %param.10) | copy-start | bytes 6148
  46.3 44.5 %copy-start.4 = (s32[128,2]{0,1:T(2,128)S(1)}, s32[128,2]{0,1:T(2,128)}, u32[]{:S(2)}) copy-start(s32[128,2]{0,1:T(2,128)} %param.9) | copy-start | bytes 3076
  46.3 44.5 %copy-start.10 = (u32[32]{0:T(128)S(1)}, u32[32]{0:T(128)}, u32[]{:S(2)}) copy-start(u32[32]{0:T(128)} %constant.57) | copy-start | bytes 388
  46.4 43.5 %all-to-all-start.1 = ((bf16[16,24,1024]{2,1,0:T(8,128)(2,1)}), bf16[16,24,1024]{2,1,0:T(8,128)(2,1)S(1)}, u32[]{:S(2)}, u32[]{:S(2)}) async-start(bf16[16,24,1024]{2,1,0:T(8,128)(2,1)} %get-tuple-element.13), calls=%async_computation.1 | async-start | bytes 1572864 | tf_op jit(solution)/shard_map/all_to_all | solution.py:68
  50.5 56.3 %all-gather.5.cloned.1.call-start = ((), (), s32[]{:S(2)}) async-start(), calls=%async_computation.6 | async-start | bytes 2359296 | tf_op jit(solution)/shard_map/all_gather | solution.py:76
  89.9 0.9 copy-start.3
  92.1 5.7 %copy-start.7 = (bf16[768,1024]{1,0:T(8,128)(2,1)S(1)}, bf16[768,1024]{1,0:T(8,128)(2,1)}, u32[]{:S(2)}) copy-start(bf16[768,1024]{1,0:T(8,128)(2,1)} %all-gather.7.cloned.1.call-done) | copy-start | bytes 4718596
  96.1 1.7 copy-start.11
  117.9 9.5 %all-to-all-start.4 = ((bf16[16,1,24]{2,1,0:T(2,128)(2,1)}), bf16[16,1,24]{2,1,0:T(2,128)(2,1)S(1)}, u32[]{:S(2)}, u32[]{:S(2)}) async-start(bf16[16,1,24]{2,1,0:T(2,128)(2,1)} %all_to_all.29), calls=%async_computation.5 | async-start | bytes 16384 | tf_op jit(solution)/shard_map/all_to_all | solution.py:97
  121.4 44.8 %reduce-scatter.2.cloned.1.call-start = ((), (), s32[]{:S(2)}) async-start(), calls=%async_computation.8 | async-start | bytes 4718592 | tf_op jit(solution)/shard_map/reduce_scatter | solution.py:83
  146.1 6.8 %copy-start.6 = (bf16[1,1024,1024]{2,1,0:T(8,128)(2,1)S(1)}, bf16[1,1024,1024]{2,1,0:T(8,128)(2,1)}, u32[]{:S(2)}) copy-start(bf16[1,1024,1024]{2,1,0:T(8,128)(2,1)} %param.11) | copy-start | bytes 6291460
  152.9 1.9 copy-start.14
  152.9 1.9 copy-start.12
  168.6 137.4 %all-to-all-start.3 = ((bf16[16,24,1024]{2,1,0:T(8,128)(2,1)}), bf16[16,24,1024]{2,1,0:T(8,128)(2,1)S(1)}, u32[]{:S(2)}, u32[]{:S(2)}) async-start(bf16[16,24,1024]{2,1,0:T(8,128)(2,1)} %bitcast.80), calls=%async_computation.4 | async-start | bytes 1572864 | tf_op jit(solution)/shard_map/all_to_all | solution.py:90
  175.0 129.6 %all-reduce.3.cloned.1.call-start = ((), (), s32[]{:S(2)}) async-start(), calls=%async_computation.9 | async-start | bytes 131072 | tf_op jit(solution)/shard_map/psum | solution.py:117
  176.2 5.2 %copy-start.9 = (bf16[768,1024]{1,0:T(8,128)(2,1)S(1)}, bf16[768,1024]{1,0:T(8,128)(2,1)}, u32[]{:S(2)}) copy-start(bf16[768,1024]{1,0:T(8,128)(2,1)} %all-gather.5.cloned.1.call-done) | copy-start | bytes 4718596
  176.2 5.2 %copy-start.15 = (bf16[768,1024]{1,0:T(8,128)(2,1)S(1)}, bf16[768,1024]{1,0:T(8,128)(2,1)}, u32[]{:S(2)}) copy-start(bf16[768,1024]{1,0:T(8,128)(2,1)} %get-tuple-element.15) | copy-start | bytes 4718596
  181.4 3.3 %copy-start.8 = (bf16[768,1024]{1,0:T(8,128)(2,1)S(1)}, bf16[768,1024]{1,0:T(8,128)(2,1)}, u32[]{:S(2)}) copy-start(bf16[768,1024]{1,0:T(8,128)(2,1)} %all-gather.7.cloned.1.call-done) | copy-start | bytes 4718596
  181.4 3.3 %copy-start.13 = (bf16[768,1024]{1,0:T(8,128)(2,1)S(1)}, bf16[768,1024]{1,0:T(8,128)(2,1)}, u32[]{:S(2)}) copy-start(bf16[768,1024]{1,0:T(8,128)(2,1)} %copy-done.12) | copy-start | bytes 4718596
Sparse Core Ops, SparseCore 0:
  46.5 9.4 all-gather.6
  90.9 15.7 all-gather.4
  158.4 7.6 reduce-scatter.1
  181.7 122.9 all-reduce.2
where the time goes:
time: 321 us; the launch traced here: 320 us
  waiting for transfers between devices  135 us (42%)
  blocking collectives  85.7 us (27%)
  matrix products  39.5 us (12%)
  local copies, waits for them, and re-layouts  22.2 us (7%)
  between operations  14.8 us (5%)
  starting transfers between devices  14.4 us (4%)
  other arithmetic  8.53 us (3%)
    psum x1, waiting for transfers between devices, local(): summed = lax.psum(partial_router, ('ep', 'dp'))  117 us
    all_gather x1, blocking collectives, local(): router_full = lax.all_gather(router_weight, 'ep', axis=0, tiled=True)  39.2 us
    all_to_all x1, blocking collectives, local(): lax.all_to_all(send_rows, 'ep', split_axis=0, concat_axis=0, tiled=True)  27.4 us
    all_to_all x1, blocking collectives, local(): lax.all_to_all(send_gates, 'ep', split_axis=0, concat_axis=0, tiled=True)  8.73 us
    reduce_scatter x1, waiting for transfers between devices, local(): lax.psum_scatter(part_rows, 'dp', scatter_dimension=0, tiled=True)  7.8 us
    dot_general x1, matrix products, expert_grads(): grad_hidden = jnp.dot(scaled, wd.T, preferred_element_type=jnp.float32)  6.77 us
    all_to_all x1, starting transfers between devices, local(): lax.all_to_all(grad_rows.astype(jnp.bfloat16).reshape(experts, cap, width...  6.43 us
  transfers between devices with their start and end apart: 7, of which 4 were waited for; matrix products, arithmetic and copies ran while one was open for 7% of the time, Pallas kernels for 0%

commit v1 on v0

--- a/solution.py
+++ b/solution.py
@@ -114,7 +114,8 @@
     router_term = jnp.dot(dense, router_full.astype(jnp.float32), precision=lax.Precision.HIGHEST)
     grad_tokens = (jnp.sum(entry_rows, axis=1) + router_term).astype(jnp.bfloat16)
     partial_router = jnp.dot(dense.T, tokens.astype(jnp.float32), precision=lax.Precision.HIGHEST)
-    summed = lax.psum(partial_router, ("ep", "dp"))
+    parts = lax.all_gather(partial_router, ("ep", "dp"), axis=0, tiled=False)
+    summed = parts.sum(axis=0)
     grad_router = lax.dynamic_slice_in_dim(summed, lax.axis_index("ep"), 1, 0)
     return (grad_tokens, grad_router, grad_gate, grad_up, grad_down)
 

time: 321 us -> 247 us (0.77)
  waiting for transfers between devices: 135 us -> 60.4 us
    psum x1 -> x0, waiting for transfers between devices: 117 us -> none  [local(): summed = lax.psum(partial_router, ('ep', 'dp'))]
    all_gather x0 -> x1, waiting for transfers between devices: none -> 42.6 us  [local(): parts = lax.all_gather(partial_router, ('ep', 'dp'), axis=0, tiled=False)]
  transfers between devices with their start and end apart: 7 -> 7, of which waited for: 4 -> 4; matrix products, arithmetic and copies ran while one was open for 7% -> 11% of each run, Pallas kernels for 0% -> 0%
where the time goes in v1:
time: 247 us; the launch traced here: 246 us
  blocking collectives  85.7 us (35%)
  waiting for transfers between devices  60.4 us (24%)
  matrix products  39.4 us (16%)
  local copies, waits for them, and re-layouts  21.4 us (9%)
  between operations  14.8 us (6%)
  starting transfers between devices  14.2 us (6%)
  other arithmetic  10.3 us (4%)
    all_gather x1, waiting for transfers between devices, local(): parts = lax.all_gather(partial_router, ('ep', 'dp'), axis=0, tiled=False)  42.6 us
    all_gather x1, blocking collectives, local(): router_full = lax.all_gather(router_weight, 'ep', axis=0, tiled=True)  39.2 us
    all_to_all x1, blocking collectives, local(): lax.all_to_all(send_rows, 'ep', split_axis=0, concat_axis=0, tiled=True)  27.4 us
    all_to_all x1, blocking collectives, local(): lax.all_to_all(send_gates, 'ep', split_axis=0, concat_axis=0, tiled=True)  8.73 us
    reduce_scatter x1, waiting for transfers between devices, local(): lax.psum_scatter(part_rows, 'dp', scatter_dimension=0, tiled=True)  6.91 us
    dot_general x1, matrix products, expert_grads(): grad_hidden = jnp.dot(scaled, wd.T, preferred_element_type=jnp.float32)  6.74 us
    all_to_all x1, starting transfers between devices, local(): lax.all_to_all(grad_rows.astype(jnp.bfloat16).reshape(experts, cap, width...  6.44 us
    unnamed x1, blocking collectives  6.04 us
  transfers between devices with their start and end apart: 7, of which 4 were waited for; matrix products, arithmetic and copies ran while one was open for 11% of the time, Pallas kernels for 0%

profile of v1, /device:TPU:1, one launch (start us, length us, event | category | flops | bytes accessed | tf_op | source)
XLA Modules:
  0.0 246.1 jit_solution(10955125048628414096)
XLA Ops:
  14.0 2.7 %gather_fusion.2 = bf16[384,1024]{1,0:T(8,128)(2,1)} fusion(bf16[128,1024]{1,0:T(8,128)(2,1)S(1)} %copy-done.1, s32[1024]{0:T(1024)S(1)} %get-tuple-element.17), kind=kCustom, calls=%fused_computation.2 | custom fusion | bytes 1574400 | tf_op jit(solution)/shard_map/gather | solution.py:61
  16.7 2.2 broadcast_select_fusion.1
  18.9 27.4 %all_to_all.35 = bf16[16,24,1024]{2,1,0:T(8,128)(2,1)} all-to-all(bf16[16,24,1024]{2,1,0:T(8,128)(2,1)S(1)} %get-tuple-element.14), channel_id=1, replica_groups=mesh['ep'=16,'dp'=2] {'ep'}, dimensions={0} | all-to-all | bytes 1572864 | tf_op jit(solution)/shard_map/all_to_all | solution.py:67
  46.4 4.1 %all-to-all-start.1 = ((bf16[16,24,1024]{2,1,0:T(8,128)(2,1)}), bf16[16,24,1024]{2,1,0:T(8,128)(2,1)S(1)}, u32[]{:S(2)}, u32[]{:S(2)}) async-start(bf16[16,24,1024]{2,1,0:T(8,128)(2,1)} %get-tuple-element.13), calls=%async_computation.1 | async-start | bytes 1572864 | tf_op jit(solution)/shard_map/all_to_all | solution.py:68
  50.5 39.2 %all-gather.1 = bf16[16,1,1024]{2,1,0:T(2,128)(2,1)S(1)} all-gather(bf16[1,1,1024]{2,1,0:T(2,128)(2,1)S(1)} %bitcast.85), channel_id=1, replica_groups=mesh['ep'=16,'dp'=2] {'ep'}, dimensions={0}, use_global_device_ids=true | all-gather | bytes 34816 | tf_op jit(solution)/shard_map/all_gather | solution.py:40
  92.1 4.0 %fusion.5 = f32[768,1024]{1,0:T(8,128)S(1)} fusion(bf16[768,1024]{1,0:T(8,128)(2,1)} %all-gather.9.cloned.1.call-done, bf16[1,1024,1024]{2,1,0:T(8,128)(2,1)} %param.11), kind=kOutput, calls=%fused_computation.17 | convolution fusion | flops 1610612736 | bytes 6815744 | tf_op jit(solution)/shard_map/dot_general | solution.py:16
  97.8 4.2 %multiply_convert_fusion = (bf16[768,1024]{1,0:T(8,128)(2,1)}, f32[768,1024]{1,0:T(8,128)}) fusion(f32[768,1024]{1,0:T(8,128)S(1)} %fusion.5, bf16[768,1024]{1,0:T(8,128)(2,1)S(1)} %copy-done.7, bf16[1,1024,1024]{2,1,0:T(8,128)(2,1)S(1)} %copy-done), kind=kOutput, calls=%fused_computation.10 | convolution fusion | flops 1615331328 | bytes 11534336 | tf_op jit(solution)/shard_map/dot_general | solution.py:17
  102.0 4.7 %all-gather.7.cloned.1.call-done = bf16[768,1024]{1,0:T(8,128)(2,1)} async-done(((bf16[384,1024]{1,0:T(8,128)(2,1)}), bf16[768,1024]{1,0:T(8,128)(2,1)}) %all-gather.7.cloned.1.call-update) | async-done | bytes 1572880 | tf_op jit(solution)/shard_map/all_gather | solution.py:76
  106.8 4.4 %fusion.1 = f32[768]{0:T(1024)S(1)} fusion(bf16[768,1024]{1,0:T(8,128)(2,1)} %all-gather.7.cloned.1.call-done, bf16[768,1024]{1,0:T(8,128)(2,1)} %get-tuple-element.15, bf16[1,1024,1024]{2,1,0:T(8,128)(2,1)} %param.13), kind=kOutput, calls=%fused_computation.9 | convolution fusion | flops 1612971264 | bytes 5245952 | tf_op jit(solution)/shard_map/dot_general | solution.py:21
  111.1 6.0 %all-reduce = bf16[768]{0:T(1024)(128)(2,1)S(1)} all-reduce(f32[768]{0:T(1024)S(1)} %fusion.1), channel_id=4, replica_groups=mesh['ep'=16,'dp'=2] {'dp'}, use_global_device_ids=true, to_apply=%region_9.10.clone | all-reduce | flops 768 | bytes 4608
  118.0 3.5 %all-to-all-start.4 = ((bf16[16,1,24]{2,1,0:T(2,128)(2,1)}), bf16[16,1,24]{2,1,0:T(2,128)(2,1)S(1)}, u32[]{:S(2)}, u32[]{:S(2)}) async-start(bf16[16,1,24]{2,1,0:T(2,128)(2,1)} %all_to_all.29), calls=%async_computation.5 | async-start | bytes 16384 | tf_op jit(solution)/shard_map/all_to_all | solution.py:97
  121.5 6.0 %all-to-all-done.4 = bf16[16,1,24]{2,1,0:T(2,128)(2,1)S(1)} async-done(((bf16[16,1,24]{2,1,0:T(2,128)(2,1)}), bf16[16,1,24]{2,1,0:T(2,128)(2,1)S(1)}, u32[]{:S(2)}, u32[]{:S(2)}) %all-to-all-start.4) | async-done | bytes 800 | tf_op jit(solution)/shard_map/all_to_all | solution.py:97
  130.1 2.7 %gather_fusion = bf16[384]{0:T(512)(128)(2,1)S(1)} fusion(bf16[256]{0:T(256)(128)(2,1)S(1)} %reshape.173, s32[1024]{0:T(1024)S(1)} %get-tuple-element.18), kind=kCustom, calls=%fused_computation | custom fusion | bytes 3072 | tf_op jit(solution)/shard_map/gather | solution.py:64
  132.9 8.7 %all_to_all.36 = bf16[16,1,24]{2,1,0:T(2,128)(2,1)S(1)} all-to-all(bf16[16,1,24]{2,1,0:T(2,128)(2,1)S(1)} %all_to_all.28), channel_id=1, replica_groups=mesh['ep'=16,'dp'=2] {'ep'}, dimensions={0} | all-to-all | bytes 1536 | tf_op jit(solution)/shard_map/all_to_all | solution.py:69
  141.8 4.3 %all-gather.2 = bf16[2,1,384]{2,1,0:T(2,128)(2,1)S(1)} all-gather(bf16[1,1,384]{2,1,0:T(2,128)(2,1)S(1)} %reshape.230), channel_id=1, replica_groups=mesh['ep'=16,'dp'=2] {'dp'}, dimensions={0}, use_global_device_ids=true | all-gather | bytes 2304 | tf_op jit(solution)/shard_map/all_gather | solution.py:77
  146.1 6.7 %multiply_convert_fusion.1 = (bf16[768,1024]{1,0:T(8,128)(2,1)S(1)}, bf16[768,1024]{1,0:T(8,128)(2,1)S(1)}) fusion(f32[768,1024]{1,0:T(8,128)} %copy-done.11, f32[768,1024]{1,0:T(8,128)} %get-tuple-element.16, bf16[1,1024,1024]{2,1,0:T(8,128)(2,1)} %param.13, bf16[768,1024]{1,0:T(8,128)(2,1)} %all-gather.7.cloned.1.call-done, f32[768]{0:T(1024)S(1)} %reshape.232), kind=kOutput, calls=%fused_computation.11 | convolution fusion | flops 1623195648 | bytes 13110272 | tf_op jit(solution)/shard_map/dot_general | solution.py:25
  154.8 3.5 %fusion.15 = f32[768,1024]{1,0:T(8,128)} fusion(f32[768,1024]{1,0:T(8,128)S(1)} %fusion.3, bf16[768,1024]{1,0:T(8,128)(2,1)S(1)} %get-tuple-element.9, bf16[1,1024,1024]{2,1,0:T(8,128)(2,1)S(1)} %copy-done), kind=kOutput, calls=%fused_computation.30 | convolution fusion | flops 1611399168 | bytes 9961472 | tf_op jit(solution)/shard_map/dot_general | solution.py:28
  159.2 6.9 %reduce-scatter.2.cloned.1.call-done = f32[384,1024]{1,0:T(8,128)} async-done(((f32[768,1024]{1,0:T(8,128)}), f32[384,1024]{1,0:T(8,128)}) %reduce-scatter.2.cloned.1.call-update) | async-done | bytes 1572880 | tf_op jit(solution)/shard_map/reduce_scatter | solution.py:83
  166.1 2.4 convert_element_type.75
  168.6 6.4 %all-to-all-start.3 = ((bf16[16,24,1024]{2,1,0:T(8,128)(2,1)}), bf16[16,24,1024]{2,1,0:T(8,128)(2,1)S(1)}, u32[]{:S(2)}, u32[]{:S(2)}) async-start(bf16[16,24,1024]{2,1,0:T(8,128)(2,1)} %bitcast.81), calls=%async_computation.4 | async-start | bytes 1572864 | tf_op jit(solution)/shard_map/all_to_all | solution.py:90
  175.0 5.2 %convert_bitcast_fusion.2 = bf16[1,1024,1024]{2,1,0:T(8,128)(2,1)} fusion(bf16[768,1024]{1,0:T(8,128)(2,1)} %all-gather.9.cloned.1.call-done, bf16[768,1024]{1,0:T(8,128)(2,1)} %copy-done.14), kind=kOutput, calls=%fused_computation.29 | convolution fusion | flops 1611661312 | bytes 5242880 | tf_op jit(solution)/shard_map/dot_general | solution.py:31
  180.3 3.2 %convert_bitcast_fusion.1 = bf16[1,1024,1024]{2,1,0:T(8,128)(2,1)} fusion(bf16[768,1024]{1,0:T(8,128)(2,1)S(1)} %copy-done.8, bf16[768,1024]{1,0:T(8,128)(2,1)S(1)} %copy-done.13), kind=kOutput, calls=%fused_computation.28 | convolution fusion | flops 1611661312 | bytes 5242880 | tf_op jit(solution)/shard_map/dot_general | solution.py:32
  183.4 3.3 %convert_bitcast_fusion = bf16[1,1024,1024]{2,1,0:T(8,128)(2,1)} fusion(bf16[768,1024]{1,0:T(8,128)(2,1)S(1)} %copy-done.15, bf16[768,1024]{1,0:T(8,128)(2,1)S(1)} %copy-done.9, f32[768]{0:T(1024)S(1)} %reshape.232), kind=kOutput, calls=%fused_computation.27 | convolution fusion | flops 1614020608 | bytes 5245952 | tf_op jit(solution)/shard_map/dot_general | solution.py:33
  186.7 42.6 %all-gather.11.cloned.1.call-done = f32[512,1024]{1,0:T(8,128)} async-done(((f32[16,1024]{1,0:T(8,128)}), f32[512,1024]{1,0:T(8,128)}) %all-gather.11.cloned.1.call-update) | async-done | bytes 2097168 | tf_op jit(solution)/shard_map/all_gather | solution.py:117
  (94 shorter events, 27.0 us)
Async XLA Ops:
  7.2 90.7 %copy-start = (bf16[1,1024,1024]{2,1,0:T(8,128)(2,1)S(1)}, bf16[1,1024,1024]{2,1,0:T(8,128)(2,1)}, u32[]{:S(2)}) copy-start(bf16[1,1024,1024]{2,1,0:T(8,128)(2,1)} %param.12) | copy-start | bytes 6291460
  7.2 4.7 %copy-start.2 = (bf16[128,1024]{1,0:T(8,128)(2,1)S(1)}, bf16[128,1024]{1,0:T(8,128)(2,1)}, u32[]{:S(2)}) copy-start(bf16[128,1024]{1,0:T(8,128)(2,1)} %param.8) | copy-start | bytes 786436
  7.2 84.9 %all-gather.9.cloned.1.call-start = ((), (), s32[]{:S(2)}) async-start(), calls=%async_computation.7 | async-start | bytes 2359296 | tf_op jit(solution)/shard_map/all_gather | solution.py:75
  11.9 2.1 copy-start.1
  18.9 31.7 %copy-start.5 = (bf16[1,1024]{1,0:T(2,128)(2,1)S(1)}, bf16[1,1024]{1,0:T(2,128)(2,1)}, u32[]{:S(2)}) copy-start(bf16[1,1024]{1,0:T(2,128)(2,1)} %param.10) | copy-start | bytes 6148
  46.3 44.5 %copy-start.4 = (s32[128,2]{0,1:T(2,128)S(1)}, s32[128,2]{0,1:T(2,128)}, u32[]{:S(2)}) copy-start(s32[128,2]{0,1:T(2,128)} %param.9) | copy-start | bytes 3076
  46.3 44.5 %copy-start.10 = (u32[32]{0:T(128)S(1)}, u32[32]{0:T(128)}, u32[]{:S(2)}) copy-start(u32[32]{0:T(128)} %constant.57) | copy-start | bytes 388
  46.4 43.5 %all-to-all-start.1 = ((bf16[16,24,1024]{2,1,0:T(8,128)(2,1)}), bf16[16,24,1024]{2,1,0:T(8,128)(2,1)S(1)}, u32[]{:S(2)}, u32[]{:S(2)}) async-start(bf16[16,24,1024]{2,1,0:T(8,128)(2,1)} %get-tuple-element.13), calls=%async_computation.1 | async-start | bytes 1572864 | tf_op jit(solution)/shard_map/all_to_all | solution.py:68
  50.5 56.3 %all-gather.7.cloned.1.call-start = ((), (), s32[]{:S(2)}) async-start(), calls=%async_computation.6 | async-start | bytes 2359296 | tf_op jit(solution)/shard_map/all_gather | solution.py:76
  89.9 0.9 copy-start.3
  92.1 5.7 %copy-start.7 = (bf16[768,1024]{1,0:T(8,128)(2,1)S(1)}, bf16[768,1024]{1,0:T(8,128)(2,1)}, u32[]{:S(2)}) copy-start(bf16[768,1024]{1,0:T(8,128)(2,1)} %all-gather.9.cloned.1.call-done) | copy-start | bytes 4718596
  96.1 1.7 copy-start.11
  118.0 9.5 %all-to-all-start.4 = ((bf16[16,1,24]{2,1,0:T(2,128)(2,1)}), bf16[16,1,24]{2,1,0:T(2,128)(2,1)S(1)}, u32[]{:S(2)}, u32[]{:S(2)}) async-start(bf16[16,1,24]{2,1,0:T(2,128)(2,1)} %all_to_all.29), calls=%async_computation.5 | async-start | bytes 16384 | tf_op jit(solution)/shard_map/all_to_all | solution.py:97
  121.4 44.7 %reduce-scatter.2.cloned.1.call-start = ((), (), s32[]{:S(2)}) async-start(), calls=%async_computation.8 | async-start | bytes 4718592 | tf_op jit(solution)/shard_map/reduce_scatter | solution.py:83
  146.1 6.8 %copy-start.6 = (bf16[1,1024,1024]{2,1,0:T(8,128)(2,1)S(1)}, bf16[1,1024,1024]{2,1,0:T(8,128)(2,1)}, u32[]{:S(2)}) copy-start(bf16[1,1024,1024]{2,1,0:T(8,128)(2,1)} %param.11) | copy-start | bytes 6291460
  152.9 1.9 copy-start.14
  152.9 1.9 copy-start.12
  158.3 71.1 %all-gather.11.cloned.1.call-start = ((), (), s32[]{:S(2)}) async-start(), calls=%async_computation.9 | async-start | bytes 2162688 | tf_op jit(solution)/shard_map/all_gather | solution.py:117
  168.6 63.1 %all-to-all-start.3 = ((bf16[16,24,1024]{2,1,0:T(8,128)(2,1)}), bf16[16,24,1024]{2,1,0:T(8,128)(2,1)S(1)}, u32[]{:S(2)}, u32[]{:S(2)}) async-start(bf16[16,24,1024]{2,1,0:T(8,128)(2,1)} %bitcast.81), calls=%async_computation.4 | async-start | bytes 1572864 | tf_op jit(solution)/shard_map/all_to_all | solution.py:90
  175.0 5.2 %copy-start.8 = (bf16[768,1024]{1,0:T(8,128)(2,1)S(1)}, bf16[768,1024]{1,0:T(8,128)(2,1)}, u32[]{:S(2)}) copy-start(bf16[768,1024]{1,0:T(8,128)(2,1)} %all-gather.9.cloned.1.call-done) | copy-start | bytes 4718596
  175.0 5.2 %copy-start.13 = (bf16[768,1024]{1,0:T(8,128)(2,1)S(1)}, bf16[768,1024]{1,0:T(8,128)(2,1)}, u32[]{:S(2)}) copy-start(bf16[768,1024]{1,0:T(8,128)(2,1)} %copy-done.12) | copy-start | bytes 4718596
  180.2 3.2 %copy-start.9 = (bf16[768,1024]{1,0:T(8,128)(2,1)S(1)}, bf16[768,1024]{1,0:T(8,128)(2,1)}, u32[]{:S(2)}) copy-start(bf16[768,1024]{1,0:T(8,128)(2,1)} %all-gather.7.cloned.1.call-done) | copy-start | bytes 4718596
  180.2 3.2 %copy-start.15 = (bf16[768,1024]{1,0:T(8,128)(2,1)S(1)}, bf16[768,1024]{1,0:T(8,128)(2,1)}, u32[]{:S(2)}) copy-start(bf16[768,1024]{1,0:T(8,128)(2,1)} %get-tuple-element.15) | copy-start | bytes 4718596
Sparse Core Ops, SparseCore 0:
  46.5 9.4 all-gather.8
  90.9 15.7 all-gather.6
  158.4 7.6 reduce-scatter.1
  169.4 59.8 all-gather.10
